TPU v7x, 128 devices: a whole 4x4x4 slice. The times are simulated.
128 devices in a mesh: chan: 16 (over z, y), seg: 4 (over x_hi, core), lag: 2 (over x_lo).
Axes of the slice: x: 4 (x_hi: 2, x_lo: 2; x = x_hi * 2 + x_lo), y: 4, z: 4, core: 2. Of those that a mesh axis runs over, the one named last changes fastest.
Arguments:
- spectra: bfloat16 [4, 10000, 2, 6144], P('seg', 'chan', None, 'lag'), may hold values from -6 to 6
- pair_local: int32 [16, 3, 256], replicated, may hold values from 0 to 624
- pair_partner: int32 [16, 3, 256], replicated, may hold values from 0 to 624, as said below
- pair_bin: int32 [16, 3, 256], replicated, may hold values from 0 to 1
- pair_owner: int32 [16, 3, 256], replicated, may hold values 0 or 1
- pair_count: int32 [16, 3], replicated, may hold values from 64 to 256, as said below
Outputs:
- stacks: float32 [10000, 2, 2048], P('chan', None, 'lag')
Inputs may be any that keep to these rules, and one draw needn't show every extreme that they name: `pair_partner`: in round 0 the two channels of a pair differ. `pair_count`: some block reaches 256 in some round.
All inputs are finite; a program needn't handle non-finite values.
Results may differ from a plain program's by a relative error of at most 0.0065.
Values may be sent and summed in bfloat16 or wider, within the bound.
No kernel may reach another device: no remote copies, remote signals or barrier semaphores. Data moves between devices by JAX's collectives and lax.ppermute only.
A program may use at most 128 MiB of HBM per device.

v0:
```python
import math
import jax
import jax.numpy as jnp
from jax import lax
from jax.sharding import PartitionSpec as P

FREQ = 6144
LAGS = 2048
ROUNDS = 3
BINS = 2


def shifted(block, axis, distance):
    devices = range(lax.axis_size(axis))
    route = [((i - distance) % len(devices), i) for i in devices]
    return lax.ppermute(block, axis, route)


def one_hot_rows(target_rows, mask_rows, total_rows):
    row_ids = jnp.arange(total_rows, dtype=jnp.int32)[:, None]
    return ((row_ids == target_rows[None, :]) & mask_rows[None, :]).astype(jnp.float32)


def bin_rows(selector, corr):
    return lax.dot_general(
        selector,
        corr,
        (((1,), (1,)), ((), ())),
        precision=lax.Precision.HIGHEST,
        preferred_element_type=jnp.float32,
    )


def per_device(spectra, pair_local, pair_partner, pair_bin, pair_owner, pair_count):
    block_index = lax.axis_index("chan")
    lag_index = lax.axis_index("lag")
    own_block = spectra[0]
    block_chans = own_block.shape[0]
    half_freq = own_block.shape[2]
    half_lags = LAGS // lax.axis_size("lag")
    total_rows = block_chans * BINS
    slot_count = pair_local.shape[2]
    freq_index = lag_index * half_freq + jnp.arange(half_freq, dtype=jnp.int32) + 1
    corr_scale = FREQ ** (-0.5)
    slot_ids = jnp.arange(slot_count, dtype=jnp.int32)
    local_stack = jnp.zeros((total_rows, half_lags), jnp.float32)
    for round_index in range(ROUNDS):
        first_index = pair_local[block_index, round_index]
        second_index = pair_partner[block_index, round_index]
        first = jnp.take(own_block, first_index, axis=0).astype(jnp.float32)
        if round_index == 0:
            second = jnp.take(own_block, second_index, axis=0).astype(jnp.float32)
        else:
            partner_block = shifted(own_block, "chan", -round_index)
            second = jnp.take(partner_block, second_index, axis=0).astype(jnp.float32)
        cross_real = first[:, 0] * second[:, 0] + first[:, 1] * second[:, 1]
        cross_imag = first[:, 1] * second[:, 0] - first[:, 0] * second[:, 1]
        cross = jnp.concatenate([cross_real, cross_imag], axis=1).astype(jnp.bfloat16)
        block_rows = math.gcd(lax.axis_size("lag") * half_lags, 512)

        def one_block(offset):
            taus = offset + jnp.arange(block_rows, dtype=jnp.int32) - LAGS // 2
            phase = jnp.mod(taus[:, None] * freq_index[None, :], 2 * FREQ)
            angle = phase.astype(jnp.float32) * (math.pi / FREQ)
            table = jnp.concatenate([jnp.cos(angle), -jnp.sin(angle)], axis=1).astype(jnp.bfloat16)
            return (
                lax.dot_general(
                    table, cross, (((1,), (1,)), ((), ())), preferred_element_type=jnp.float32
                )
                * corr_scale
            )

        offsets = (
            jnp.arange(lax.axis_size("lag") * half_lags // block_rows, dtype=jnp.int32) * block_rows
        )
        corr = lax.psum_scatter(
            lax.map(one_block, offsets).reshape(lax.axis_size("lag") * half_lags, slot_count),
            "lag",
            scatter_dimension=0,
            tiled=True,
        )
        live = slot_ids < pair_count[block_index, round_index]
        owners = pair_owner[block_index, round_index]
        bins_now = pair_bin[block_index, round_index]
        own_rows = jnp.where(owners == 0, first_index, second_index) * BINS + bins_now
        if round_index == 0:
            local_stack = bin_rows(one_hot_rows(own_rows, live, total_rows), corr)
        else:
            mine_rows = first_index * BINS + bins_now
            local_stack = local_stack + bin_rows(
                one_hot_rows(mine_rows, live & (owners == 0), total_rows), corr
            )
            partner_rows = second_index * BINS + bins_now
            partner_stack = bin_rows(
                one_hot_rows(partner_rows, live & (owners == 1), total_rows), corr
            )
            local_stack = local_stack + shifted(partner_stack, "chan", round_index)
    local_stack = lax.psum(local_stack, "seg")
    return local_stack.reshape(block_chans, BINS, half_lags)


def solution(mesh):
    return jax.shard_map(
        per_device,
        mesh=mesh,
        in_specs=(P("seg", "chan", None, "lag"), P(), P(), P(), P(), P()),
        out_specs=P("chan", None, "lag"),
        check_vma=False,
    )
```

profile of v0, /device:TPU:1, one launch (start us, length us, event | category | flops | bytes accessed | tf_op | source)
XLA Modules:
  0.0 1053.6 jit_solution(12858665571062625390)
XLA Ops:
  6.5 7.0 collective-permute-start
  16.7 16.3 %gather_fusion.2 = bf16[256,2,3072]{2,1,0:T(2,128)(2,1)S(1)} fusion(bf16[625,2,3072]{2,1,0:T(2,128)(2,1)} %bitcast.81, s32[1024]{0:T(1024)S(1)} %pad_clamp_fusion.3), kind=kCustom, calls=%fused_computation.2.clone | custom fusion | bytes 6292480 | tf_op jit(solution)/shard_map/jit(_take)/gather | solution.py:50
  33.1 1.3 compare_reduce_fusion.3
  35.0 16.2 %gather_fusion = bf16[256,2,3072]{2,1,0:T(2,128)(2,1)} fusion(bf16[625,2,3072]{2,1,0:T(2,128)(2,1)} %bitcast.82, s32[1024]{0:T(1024)S(1)} %get-tuple-element.328), kind=kCustom, calls=%fused_computation.clone | custom fusion | bytes 6292480 | tf_op jit(solution)/shard_map/jit(_take)/gather | solution.py:50
  51.2 16.5 %gather_fusion.1 = bf16[256,2,3072]{2,1,0:T(2,128)(2,1)} fusion(bf16[625,2,3072]{2,1,0:T(2,128)(2,1)} %bitcast.83, s32[1024]{0:T(1024)S(1)} %get-tuple-element.327), kind=kCustom, calls=%fused_computation.1.clone | custom fusion | bytes 6292480 | tf_op jit(solution)/shard_map/jit(_take)/gather | solution.py:52
  68.2 16.6 %gather_fusion.4 = bf16[256,2,3072]{2,1,0:T(2,128)(2,1)} fusion(bf16[625,2,3072]{2,1,0:T(2,128)(2,1)} %bitcast.84, s32[1024]{0:T(1024)S(1)} %pad_clamp_fusion.1), kind=kCustom, calls=%fused_computation.4.clone | custom fusion | bytes 6292480 | tf_op jit(solution)/shard_map/jit(_take)/gather | solution.py:50
  85.0 5.5 fusion.65
  90.5 5.5 fusion.63
  96.0 5.6 fusion.67
  101.6 240.8 %collective-permute-done = bf16[625,2,3072]{2,1,0:T(2,128)(2,1)} collective-permute-done((bf16[625,2,3072]{2,1,0:T(2,128)(2,1)}, bf16[625,2,3072]{2,1,0:T(2,128)(2,1)}, u32[]{:S(2)}, u32[]{:S(2)}) %collective-permute-start) | collective-permute-done | bytes 7680032 | tf_op jit(solution)/shard_map/ppermute | solution.py:16
  342.4 16.5 %gather_fusion.3 = bf16[256,2,3072]{2,1,0:T(2,128)(2,1)} fusion(bf16[625,2,3072]{2,1,0:T(2,128)(2,1)} %collective-permute-done, s32[1024]{0:T(1024)S(1)} %pad_clamp_fusion.2), kind=kCustom, calls=%fused_computation.3.clone | custom fusion | bytes 6292480 | tf_op jit(solution)/shard_map/jit(_take)/gather | solution.py:55
  358.9 7.6 fusion.66
  366.6 12.3 %add_convert_fusion.1 = (bf16[256,1,3072]{2,1,0:T(2,128)(2,1)S(1)}, bf16[256,1,3072]{2,1,0:T(2,128)(2,1)S(1)}) fusion(f32[256,2,3072]{2,1,0:T(2,128)} %fusion.66, f32[256,2,3072]{2,1,0:T(2,128)S(1)} %bitcast.78), kind=kLoop, calls=%fused_computation.85 | loop fusion | flops 6291456 | bytes 15728640 | tf_op jit(solution)/shard_map/convert.13
  379.8 1.9 pad_maximum_fusion.1
  381.9 118.2 %while.40 = (s32[]{:T(128)}, f32[4,512,256]{2,1,0:T(8,128)S(1)}, s32[4]{0:T(128)S(1)}, bf16[256,6144]{1,0:T(8,128)(2,1)}, s32[]{:T(128)}, /*index=5*/s32[]{:T(128)}) while((s32[]{:T(128)}, f32[4,512,256]{2,1,0:T(8,128)S(1)}, s32[4]{0:T(128)S(1)}, bf16[256,6144]{1,0:T(8,128)(2,1)}, s32[]{:T(128)}, /*index=5*/s32[]{:T(128)}) %tuple.118), condition=%wide.region_4.6_spmd.clone, body=%wide.region_3.5_spmd.clone.sunk | while | flops 1642208256 | bytes 28864632 | solution.py:77
  383.3 26.3 %cosine_convert_fusion.7 = (bf16[512,3072]{1,0:T(8,128)(2,1)S(1)}, bf16[512,3072]{1,0:T(8,128)(2,1)S(1)}) fusion(s32[3072]{0:T(1024)S(1)} %add_add_fusion.15, s32[512]{0:T(512)S(1)} %add_add_fusion.16), kind=kLoop, calls=%fused_computation.36.clone.1 | loop fusion | flops 18874368 | bytes 6305792 | tf_op jit(solution)/shard_map/convert.2
  409.6 1.8 fusion.119
  412.8 26.3 %cosine_convert_fusion.7 = (bf16[512,3072]{1,0:T(8,128)(2,1)S(1)}, bf16[512,3072]{1,0:T(8,128)(2,1)S(1)}) fusion(s32[3072]{0:T(1024)S(1)} %add_add_fusion.15, s32[512]{0:T(512)S(1)} %add_add_fusion.16), kind=kLoop, calls=%fused_computation.36.clone.1 | loop fusion | flops 18874368 | bytes 6305792 | tf_op jit(solution)/shard_map/convert.2
  439.2 1.8 fusion.119
  442.4 26.3 %cosine_convert_fusion.7 = (bf16[512,3072]{1,0:T(8,128)(2,1)S(1)}, bf16[512,3072]{1,0:T(8,128)(2,1)S(1)}) fusion(s32[3072]{0:T(1024)S(1)} %add_add_fusion.15, s32[512]{0:T(512)S(1)} %add_add_fusion.16), kind=kLoop, calls=%fused_computation.36.clone.1 | loop fusion | flops 18874368 | bytes 6305792 | tf_op jit(solution)/shard_map/convert.2
  468.7 1.8 fusion.119
  471.9 26.3 %cosine_convert_fusion.7 = (bf16[512,3072]{1,0:T(8,128)(2,1)S(1)}, bf16[512,3072]{1,0:T(8,128)(2,1)S(1)}) fusion(s32[3072]{0:T(1024)S(1)} %add_add_fusion.15, s32[512]{0:T(512)S(1)} %add_add_fusion.16), kind=kLoop, calls=%fused_computation.36.clone.1 | loop fusion | flops 18874368 | bytes 6305792 | tf_op jit(solution)/shard_map/convert.2
  498.3 1.8 fusion.119
  500.1 1.4 copy-done.4
  501.7 16.7 %gather_fusion.5 = bf16[256,2,3072]{2,1,0:T(2,128)(2,1)} fusion(bf16[625,2,3072]{2,1,0:T(2,128)(2,1)} %collective-permute-done.2, s32[1024]{0:T(1024)S(1)} %pad_clamp_fusion), kind=kCustom, calls=%fused_computation.5.clone | custom fusion | bytes 6292480 | tf_op jit(solution)/shard_map/jit(_take)/gather | solution.py:55
  518.4 7.6 fusion.68
  526.0 12.4 %add_convert_fusion = (bf16[256,1,3072]{2,1,0:T(2,128)(2,1)S(1)}, bf16[256,1,3072]{2,1,0:T(2,128)(2,1)S(1)}) fusion(f32[256,2,3072]{2,1,0:T(2,128)} %fusion.68, f32[256,2,3072]{2,1,0:T(2,128)S(1)} %bitcast.76), kind=kLoop, calls=%fused_computation.83 | loop fusion | flops 6291456 | bytes 15728640 | tf_op jit(solution)/shard_map/convert.9
  539.4 1.9 pad_maximum_fusion.2
  541.3 1.5 broadcast.191.clone
  542.8 121.2 %while.41 = (s32[]{:T(128)}, f32[4,512,256]{2,1,0:T(8,128)}, s32[4]{0:T(128)S(1)}, bf16[256,6144]{1,0:T(8,128)(2,1)}, s32[]{:T(128)}, /*index=5*/s32[]{:T(128)}) while((s32[]{:T(128)}, f32[4,512,256]{2,1,0:T(8,128)}, s32[4]{0:T(128)S(1)}, bf16[256,6144]{1,0:T(8,128)(2,1)}, s32[]{:T(128)}, /*index=5*/s32[]{:T(128)}) %tuple.132), condition=%wide.region_7.9_spmd.clone, body=%wide.region_6.8_spmd.clone.sunk | while | flops 1642208256 | bytes 28865140 | solution.py:77
  544.4 26.3 %cosine_convert_fusion.8 = (bf16[512,3072]{1,0:T(8,128)(2,1)S(1)}, bf16[512,3072]{1,0:T(8,128)(2,1)S(1)}) fusion(s32[3072]{0:T(1024)S(1)} %add_add_fusion.17, s32[512]{0:T(512)S(1)} %add_add_fusion.18), kind=kLoop, calls=%fused_computation.55.clone.1 | loop fusion | flops 18874368 | bytes 6305792 | tf_op jit(solution)/shard_map/convert.4
  570.7 2.6 fusion.122
  574.6 26.3 %cosine_convert_fusion.8 = (bf16[512,3072]{1,0:T(8,128)(2,1)S(1)}, bf16[512,3072]{1,0:T(8,128)(2,1)S(1)}) fusion(s32[3072]{0:T(1024)S(1)} %add_add_fusion.17, s32[512]{0:T(512)S(1)} %add_add_fusion.18), kind=kLoop, calls=%fused_computation.55.clone.1 | loop fusion | flops 18874368 | bytes 6305792 | tf_op jit(solution)/shard_map/convert.4
  601.0 2.6 fusion.122
  604.8 26.3 %cosine_convert_fusion.8 = (bf16[512,3072]{1,0:T(8,128)(2,1)S(1)}, bf16[512,3072]{1,0:T(8,128)(2,1)S(1)}) fusion(s32[3072]{0:T(1024)S(1)} %add_add_fusion.17, s32[512]{0:T(512)S(1)} %add_add_fusion.18), kind=kLoop, calls=%fused_computation.55.clone.1 | loop fusion | flops 18874368 | bytes 6305792 | tf_op jit(solution)/shard_map/convert.4
  631.2 2.6 fusion.122
  635.0 26.3 %cosine_convert_fusion.8 = (bf16[512,3072]{1,0:T(8,128)(2,1)S(1)}, bf16[512,3072]{1,0:T(8,128)(2,1)S(1)}) fusion(s32[3072]{0:T(1024)S(1)} %add_add_fusion.17, s32[512]{0:T(512)S(1)} %add_add_fusion.18), kind=kLoop, calls=%fused_computation.55.clone.1 | loop fusion | flops 18874368 | bytes 6305792 | tf_op jit(solution)/shard_map/convert.4
  661.4 2.6 fusion.122
  664.1 2.8 fusion.64
  667.0 12.0 %add_convert_fusion.2 = (bf16[256,1,3072]{2,1,0:T(2,128)(2,1)S(1)}, bf16[256,1,3072]{2,1,0:T(2,128)(2,1)S(1)}) fusion(f32[256,2,3072]{2,1,0:T(2,128)S(1)} %fusion.64, f32[256,2,3072]{2,1,0:T(2,128)} %fusion.63), kind=kLoop, calls=%fused_computation.87 | loop fusion | flops 6291456 | bytes 15728640 | tf_op jit(solution)/shard_map/convert.17
  682.1 1.9 pad_maximum_fusion
  684.0 5.8 fusion.75
  689.8 11.1 %reduce-scatter.8.cloned.1.call-done = f32[1024,256]{1,0:T(8,128)} async-done(((f32[2048,256]{1,0:T(8,128)}), f32[1024,256]{1,0:T(8,128)}) %reduce-scatter.8.cloned.1.call-update) | async-done | bytes 1048592 | tf_op jit(solution)/shard_map/reduce_scatter | solution.py:76
  701.0 5.7 fusion.81
  706.7 2.7 collective-permute-start.3
  709.6 117.7 %while.39 = (s32[]{:T(128)}, f32[4,512,256]{2,1,0:T(8,128)S(1)}, s32[4]{0:T(128)S(1)}, bf16[256,6144]{1,0:T(8,128)(2,1)}, s32[]{:T(128)}, /*index=5*/s32[]{:T(128)}) while((s32[]{:T(128)}, f32[4,512,256]{2,1,0:T(8,128)S(1)}, s32[4]{0:T(128)S(1)}, bf16[256,6144]{1,0:T(8,128)(2,1)}, s32[]{:T(128)}, /*index=5*/s32[]{:T(128)}) %tuple.133), condition=%wide.region_1.3_spmd.clone, body=%wide.region_0.0_spmd.clone.sunk | while | flops 1642208256 | bytes 28864632 | solution.py:77
  710.9 26.3 %cosine_convert_fusion.6 = (bf16[512,3072]{1,0:T(8,128)(2,1)S(1)}, bf16[512,3072]{1,0:T(8,128)(2,1)S(1)}) fusion(s32[3072]{0:T(1024)S(1)} %add_add_fusion.13, s32[512]{0:T(512)S(1)} %add_add_fusion.14), kind=kLoop, calls=%fused_computation.17.clone.1 | loop fusion | flops 18874368 | bytes 6305792 | tf_op jit(solution)/shard_map/convert
  737.2 1.8 fusion.116
  740.3 26.3 %cosine_convert_fusion.6 = (bf16[512,3072]{1,0:T(8,128)(2,1)S(1)}, bf16[512,3072]{1,0:T(8,128)(2,1)S(1)}) fusion(s32[3072]{0:T(1024)S(1)} %add_add_fusion.13, s32[512]{0:T(512)S(1)} %add_add_fusion.14), kind=kLoop, calls=%fused_computation.17.clone.1 | loop fusion | flops 18874368 | bytes 6305792 | tf_op jit(solution)/shard_map/convert
  766.6 1.8 fusion.116
  769.7 26.3 %cosine_convert_fusion.6 = (bf16[512,3072]{1,0:T(8,128)(2,1)S(1)}, bf16[512,3072]{1,0:T(8,128)(2,1)S(1)}) fusion(s32[3072]{0:T(1024)S(1)} %add_add_fusion.13, s32[512]{0:T(512)S(1)} %add_add_fusion.14), kind=kLoop, calls=%fused_computation.17.clone.1 | loop fusion | flops 18874368 | bytes 6305792 | tf_op jit(solution)/shard_map/convert
  796.1 1.8 fusion.116
  799.2 26.3 %cosine_convert_fusion.6 = (bf16[512,3072]{1,0:T(8,128)(2,1)S(1)}, bf16[512,3072]{1,0:T(8,128)(2,1)S(1)}) fusion(s32[3072]{0:T(1024)S(1)} %add_add_fusion.13, s32[512]{0:T(512)S(1)} %add_add_fusion.14), kind=kLoop, calls=%fused_computation.17.clone.1 | loop fusion | flops 18874368 | bytes 6305792 | tf_op jit(solution)/shard_map/convert
  825.5 1.8 fusion.116
  827.4 1.3 copy-done.3
  829.6 1.3 fusion.94
  830.8 32.4 %reduce-scatter.4.cloned.1.call-done = f32[1024,256]{1,0:T(8,128)} async-done(((f32[2048,256]{1,0:T(8,128)}), f32[1024,256]{1,0:T(8,128)}) %reduce-scatter.4.cloned.1.call-update) | async-done | bytes 1048592 | tf_op jit(solution)/shard_map/reduce_scatter | solution.py:76
  863.3 3.6 fusion.70
  866.9 2.3 fusion.78
  869.1 47.5 %collective-permute-done.3 = f32[1250,1024]{1,0:T(8,128)} collective-permute-done((f32[1250,1024]{1,0:T(8,128)}, f32[1250,1024]{1,0:T(8,128)}, u32[]{:S(2)}, u32[]{:S(2)}) %collective-permute-start.3) | collective-permute-done | bytes 5120032 | tf_op jit(solution)/shard_map/ppermute | solution.py:16
  916.6 9.4 add_add_fusion.6
  926.0 7.3 reshape.172
  933.3 106.7 %all-reduce.2.cloned.1.call-done = f32[625,2,1024]{2,1,0:T(2,128)} async-done(((f32[625,2,1024]{2,1,0:T(2,128)}), f32[625,2,1024]{2,1,0:T(2,128)}) %all-reduce.2.cloned.1.call-update) | async-done | bytes 5120016 | tf_op jit(solution)/shard_map/psum | solution.py:98
  1040.1 6.5 copy.63
  (134 shorter events, 26.1 us)
Async XLA Ops:
  6.5 677.5 %reduce-scatter.6.cloned.1.call-start = ((), (), s32[]{:S(2)}) async-start(), calls=%async_computation.4 | async-start | bytes 3145728 | tf_op jit(solution)/shard_map/reduce_scatter | solution.py:76
  6.5 335.9 %collective-permute-start = (bf16[625,2,3072]{2,1,0:T(2,128)(2,1)}, bf16[625,2,3072]{2,1,0:T(2,128)(2,1)}, u32[]{:S(2)}, u32[]{:S(2)}) collective-permute-start(bf16[625,2,3072]{2,1,0:T(2,128)(2,1)} %bitcast.79), channel_id=1, source_target_pairs={{8,0},{16,8},{24,16},{32,24},{40,32},{48,40},{56,48},{64,56},{72,6... | collective-permute-start | bytes 23040008 | tf_op jit(solution)/shard_map/ppermute | solution.py:16
  13.6 488.1 %collective-permute-start.2 = (bf16[625,2,3072]{2,1,0:T(2,128)(2,1)}, bf16[625,2,3072]{2,1,0:T(2,128)(2,1)}, u32[]{:S(2)}, u32[]{:S(2)}) collective-permute-start(bf16[625,2,3072]{2,1,0:T(2,128)(2,1)} %bitcast.80), channel_id=1, source_target_pairs={{16,0},{24,8},{32,16},{40,24},{48,32},{56,40},{64,48},{72,56},{80,... | collective-permute-start | bytes 23040008 | tf_op jit(solution)/shard_map/ppermute | solution.py:16
  85.0 5.5 copy-start.1
  90.5 5.5 copy-start.2
  342.4 24.1 %slice-start.2 = ((s8[6291456]{0:T(1024)(128)(4,1)}), s8[2097152]{0:T(1024)(128)(4,1)S(1)}, s32[]{:S(2)}) async-start(s8[6291456]{0:T(1024)(128)(4,1)} %bitcast.77), calls=%async_computation.9 | async-start | bytes 4194304
  358.9 7.6 slice-start.3
  383.3 26.3 %copy-start.8 = (bf16[256,6144]{1,0:T(8,128)(2,1)S(1)}, bf16[256,6144]{1,0:T(8,128)(2,1)}, u32[]{:S(2)}) copy-start(bf16[256,6144]{1,0:T(8,128)(2,1)} %get-tuple-element.467) | copy-start | bytes 9437188 | tf_op jit(solution)/shard_map/while
  412.8 26.3 %copy-start.8 = (bf16[256,6144]{1,0:T(8,128)(2,1)S(1)}, bf16[256,6144]{1,0:T(8,128)(2,1)}, u32[]{:S(2)}) copy-start(bf16[256,6144]{1,0:T(8,128)(2,1)} %get-tuple-element.467) | copy-start | bytes 9437188 | tf_op jit(solution)/shard_map/while
  442.4 26.3 %copy-start.8 = (bf16[256,6144]{1,0:T(8,128)(2,1)S(1)}, bf16[256,6144]{1,0:T(8,128)(2,1)}, u32[]{:S(2)}) copy-start(bf16[256,6144]{1,0:T(8,128)(2,1)} %get-tuple-element.467) | copy-start | bytes 9437188 | tf_op jit(solution)/shard_map/while
  471.9 26.3 %copy-start.8 = (bf16[256,6144]{1,0:T(8,128)(2,1)S(1)}, bf16[256,6144]{1,0:T(8,128)(2,1)}, u32[]{:S(2)}) copy-start(bf16[256,6144]{1,0:T(8,128)(2,1)} %get-tuple-element.467) | copy-start | bytes 9437188 | tf_op jit(solution)/shard_map/while
  500.1 1.4 copy-start.4
  501.6 199.4 %reduce-scatter.8.cloned.1.call-start = ((), (), s32[]{:S(2)}) async-start(), calls=%async_computation.5 | async-start | bytes 3145728 | tf_op jit(solution)/shard_map/reduce_scatter | solution.py:76
  501.7 24.3 %slice-start = ((s8[6291456]{0:T(1024)(128)(4,1)}), s8[2097152]{0:T(1024)(128)(4,1)S(1)}, s32[]{:S(2)}) async-start(s8[6291456]{0:T(1024)(128)(4,1)} %bitcast.75), calls=%async_computation.7 | async-start | bytes 4194304
  518.4 7.6 slice-start.1
  542.8 121.3 %copy-start = (bf16[256,2,3072]{2,1,0:T(2,128)(2,1)S(1)}, bf16[256,2,3072]{2,1,0:T(2,128)(2,1)}, u32[]{:S(2)}) copy-start(bf16[256,2,3072]{2,1,0:T(2,128)(2,1)} %gather_fusion.1) | copy-start | bytes 9437188
  544.4 26.3 %copy-start.9 = (bf16[256,6144]{1,0:T(8,128)(2,1)S(1)}, bf16[256,6144]{1,0:T(8,128)(2,1)}, u32[]{:S(2)}) copy-start(bf16[256,6144]{1,0:T(8,128)(2,1)} %get-tuple-element.449) | copy-start | bytes 9437188 | tf_op jit(solution)/shard_map/while
  574.6 26.3 %copy-start.9 = (bf16[256,6144]{1,0:T(8,128)(2,1)S(1)}, bf16[256,6144]{1,0:T(8,128)(2,1)}, u32[]{:S(2)}) copy-start(bf16[256,6144]{1,0:T(8,128)(2,1)} %get-tuple-element.449) | copy-start | bytes 9437188 | tf_op jit(solution)/shard_map/while
  604.8 26.3 %copy-start.9 = (bf16[256,6144]{1,0:T(8,128)(2,1)S(1)}, bf16[256,6144]{1,0:T(8,128)(2,1)}, u32[]{:S(2)}) copy-start(bf16[256,6144]{1,0:T(8,128)(2,1)} %get-tuple-element.449) | copy-start | bytes 9437188 | tf_op jit(solution)/shard_map/while
  635.0 26.3 %copy-start.9 = (bf16[256,6144]{1,0:T(8,128)(2,1)S(1)}, bf16[256,6144]{1,0:T(8,128)(2,1)}, u32[]{:S(2)}) copy-start(bf16[256,6144]{1,0:T(8,128)(2,1)} %get-tuple-element.449) | copy-start | bytes 9437188 | tf_op jit(solution)/shard_map/while
  664.0 199.2 %reduce-scatter.4.cloned.1.call-start = ((), (), s32[]{:S(2)}) async-start(), calls=%async_computation.3 | async-start | bytes 3145728 | tf_op jit(solution)/shard_map/reduce_scatter | solution.py:76
  679.5 0.7 copy-start.15
  689.8 179.3 %collective-permute-start.1 = (f32[1250,1024]{1,0:T(8,128)}, f32[1250,1024]{1,0:T(8,128)}, u32[]{:S(2)}, u32[]{:S(2)}) collective-permute-start(f32[1250,1024]{1,0:T(8,128)} %fusion.75), channel_id=1, source_target_pairs={{120,0},{0,8},{8,16},{16,24},{24,32},{32,40},{40,48},{48,56},{56,6... | collective-permute-start | bytes 15360008 | tf_op jit(solution)/shard_map/ppermute | solution.py:16
  706.7 209.9 %collective-permute-start.3 = (f32[1250,1024]{1,0:T(8,128)}, f32[1250,1024]{1,0:T(8,128)}, u32[]{:S(2)}, u32[]{:S(2)}) collective-permute-start(f32[1250,1024]{1,0:T(8,128)} %fusion.81), channel_id=1, source_target_pairs={{112,0},{120,8},{0,16},{8,24},{16,32},{24,40},{32,48},{40,56},{48,... | collective-permute-start | bytes 15360008 | tf_op jit(solution)/shard_map/ppermute | solution.py:16
  709.6 120.0 %copy-start.13 = (pred[256]{0:T(512)(128)(4,1)S(1)}, pred[256]{0:T(512)(128)(4,1)}, u32[]{:S(2)}) copy-start(pred[256]{0:T(512)(128)(4,1)} %get-tuple-element.249) | copy-start | bytes 772
  709.6 120.0 %copy-start.14 = (pred[256]{0:T(512)(128)(4,1)S(1)}, pred[256]{0:T(512)(128)(4,1)}, u32[]{:S(2)}) copy-start(pred[256]{0:T(512)(128)(4,1)} %get-tuple-element.253) | copy-start | bytes 772
  709.6 153.6 %copy-start.11 = (s32[256]{0:T(256)S(1)}, s32[256]{0:T(256)}, u32[]{:S(2)}) copy-start(s32[256]{0:T(256)} %get-tuple-element.312) | copy-start | bytes 3076
  710.9 26.3 %copy-start.7 = (bf16[256,6144]{1,0:T(8,128)(2,1)S(1)}, bf16[256,6144]{1,0:T(8,128)(2,1)}, u32[]{:S(2)}) copy-start(bf16[256,6144]{1,0:T(8,128)(2,1)} %get-tuple-element.485) | copy-start | bytes 9437188 | tf_op jit(solution)/shard_map/while
  740.3 26.3 %copy-start.7 = (bf16[256,6144]{1,0:T(8,128)(2,1)S(1)}, bf16[256,6144]{1,0:T(8,128)(2,1)}, u32[]{:S(2)}) copy-start(bf16[256,6144]{1,0:T(8,128)(2,1)} %get-tuple-element.485) | copy-start | bytes 9437188 | tf_op jit(solution)/shard_map/while
  769.7 26.3 %copy-start.7 = (bf16[256,6144]{1,0:T(8,128)(2,1)S(1)}, bf16[256,6144]{1,0:T(8,128)(2,1)}, u32[]{:S(2)}) copy-start(bf16[256,6144]{1,0:T(8,128)(2,1)} %get-tuple-element.485) | copy-start | bytes 9437188 | tf_op jit(solution)/shard_map/while
  799.2 26.3 %copy-start.7 = (bf16[256,6144]{1,0:T(8,128)(2,1)S(1)}, bf16[256,6144]{1,0:T(8,128)(2,1)}, u32[]{:S(2)}) copy-start(bf16[256,6144]{1,0:T(8,128)(2,1)} %get-tuple-element.485) | copy-start | bytes 9437188 | tf_op jit(solution)/shard_map/while
  827.4 1.3 copy-start.3
  828.7 211.4 %all-reduce.2.cloned.1.call-start = ((), (), s32[]{:S(2)}) async-start(), calls=%async_computation.6 | async-start | bytes 10240000 | tf_op jit(solution)/shard_map/psum | solution.py:98
  863.3 3.6 copy-start.6
  863.3 3.6 copy-start.10
  866.8 49.8 %copy-start.5 = (f32[1024,256]{1,0:T(8,128)S(1)}, f32[1024,256]{1,0:T(8,128)}, u32[]{:S(2)}) copy-start(f32[1024,256]{1,0:T(8,128)} %reduce-scatter.6.cloned.1.call-done) | copy-start | bytes 3145732
  866.9 49.7 %copy-start.12 = (s32[256]{0:T(256)S(1)}, s32[256]{0:T(256)}, u32[]{:S(2)}) copy-start(s32[256]{0:T(256)} %get-tuple-element.308) | copy-start | bytes 3076
Sparse Core Ops, SparseCore 0:
  501.7 36.7 reduce-scatter.5
  664.2 36.7 reduce-scatter.7
  828.8 34.3 reduce-scatter.3
  933.5 106.5 all-reduce.1
where the time goes:
time: 1060 us; the launch traced here: 1050 us
  waiting for transfers between devices  439 us (41%)
  other arithmetic  407 us (38%)
  local copies, waits for them, and re-layouts  131 us (12%)
  matrix products  51.9 us (5%)
  between operations  13.9 us (1%)
    another operation x15, other arithmetic  353 us
    ppermute x4, waiting for transfers between devices, shifted(): return lax.ppermute(block, axis, route)  288 us
    psum x1, waiting for transfers between devices, per_device(): local_stack = lax.psum(local_stack, 'seg')  107 us
    gather x3, local copies, waits for them, and re-layouts, per_device(): first = jnp.take(own_block, first_index, axis=0).astype(jnp.float32)  49.2 us
    reduce_scatter x3, waiting for transfers between devices, per_device(): lax.psum_scatter(lax.map(one_block, offsets).reshape(lax.axis_size('lag')...  43.5 us
    gather x2, local copies, waits for them, and re-layouts, per_device(): second = jnp.take(partner_block, second_index, axis=0).astype(jnp.float32)  33.3 us
    dot_general x5, matrix products, bin_rows(): lax.dot_general(selector, corr, (((1,), (1,)), ((), ())), precision=lax.P...  26.8 us
    dot_general x12, matrix products, one_block(): lax.dot_general(table, cross, (((1,), (1,)), ((), ())), preferred_element...  25.1 us
  transfers between devices with their start and end apart: 8, of which 5 were waited for; matrix products, arithmetic and copies ran while one was open for 53% of the time, Pallas kernels for 0%

commit v1 on v0

--- a/solution.py
+++ b/solution.py
@@ -95,7 +95,7 @@
                 one_hot_rows(partner_rows, live & (owners == 1), total_rows), corr
             )
             local_stack = local_stack + shifted(partner_stack, "chan", round_index)
-    local_stack = lax.psum(local_stack, "seg")
+    local_stack = jnp.sum(lax.all_gather(local_stack, "seg"), axis=0)
     return local_stack.reshape(block_chans, BINS, half_lags)
 
 

time: 1060 us -> 1090 us (1.028)
  waiting for transfers between devices: 439 us -> 464 us
    all_gather x0 -> x1, waiting for transfers between devices: none -> 132 us  [per_device(): local_stack = jnp.sum(lax.all_gather(local_stack, 'seg'), axis=0)]
    psum x1 -> x0, waiting for transfers between devices: 107 us -> none  [per_device(): local_stack = lax.psum(local_stack, 'seg')]
  transfers between devices with their start and end apart: 8 -> 8, of which waited for: 5 -> 5; matrix products, arithmetic and copies ran while one was open for 53% -> 52% of each run, Pallas kernels for 0% -> 0%
where the time goes in v1:
time: 1090 us; the launch traced here: 1080 us
  waiting for transfers between devices  464 us (43%)
  other arithmetic  417 us (38%)
  local copies, waits for them, and re-layouts  124 us (11%)
  matrix products  51.9 us (5%)
  between operations  13.9 us (1%)
    another operation x15, other arithmetic  353 us
    ppermute x4, waiting for transfers between devices, shifted(): return lax.ppermute(block, axis, route)  288 us
    all_gather x1, waiting for transfers between devices, per_device(): local_stack = jnp.sum(lax.all_gather(local_stack, 'seg'), axis=0)  132 us
    gather x3, local copies, waits for them, and re-layouts, per_device(): first = jnp.take(own_block, first_index, axis=0).astype(jnp.float32)  49.2 us
    reduce_scatter x3, waiting for transfers between devices, per_device(): lax.psum_scatter(lax.map(one_block, offsets).reshape(lax.axis_size('lag')...  43.5 us
    gather x2, local copies, waits for them, and re-layouts, per_device(): second = jnp.take(partner_block, second_index, axis=0).astype(jnp.float32)  33.3 us
    dot_general x5, matrix products, bin_rows(): lax.dot_general(selector, corr, (((1,), (1,)), ((), ())), precision=lax.P...  26.7 us
    dot_general x12, matrix products, one_block(): lax.dot_general(table, cross, (((1,), (1,)), ((), ())), preferred_element...  25.1 us
  transfers between devices with their start and end apart: 8, of which 5 were waited for; matrix products, arithmetic and copies ran while one was open for 52% of the time, Pallas kernels for 0%

profile of v1, /device:TPU:1, one launch (start us, length us, event | category | flops | bytes accessed | tf_op | source)
XLA Modules:
  0.0 1082.7 jit_solution(11990625993006909180)
XLA Ops:
  6.5 7.0 collective-permute-start
  16.7 16.3 %gather_fusion.2 = bf16[256,2,3072]{2,1,0:T(2,128)(2,1)S(1)} fusion(bf16[625,2,3072]{2,1,0:T(2,128)(2,1)} %bitcast.83, s32[1024]{0:T(1024)S(1)} %pad_clamp_fusion.3), kind=kCustom, calls=%fused_computation.2.clone | custom fusion | bytes 6292480 | tf_op jit(solution)/shard_map/jit(_take)/gather | solution.py:50
  33.1 1.3 compare_reduce_fusion.3
  35.0 16.2 %gather_fusion = bf16[256,2,3072]{2,1,0:T(2,128)(2,1)} fusion(bf16[625,2,3072]{2,1,0:T(2,128)(2,1)} %bitcast.84, s32[1024]{0:T(1024)S(1)} %get-tuple-element.328), kind=kCustom, calls=%fused_computation.clone | custom fusion | bytes 6292480 | tf_op jit(solution)/shard_map/jit(_take)/gather | solution.py:50
  51.2 16.5 %gather_fusion.1 = bf16[256,2,3072]{2,1,0:T(2,128)(2,1)} fusion(bf16[625,2,3072]{2,1,0:T(2,128)(2,1)} %bitcast.85, s32[1024]{0:T(1024)S(1)} %get-tuple-element.327), kind=kCustom, calls=%fused_computation.1.clone | custom fusion | bytes 6292480 | tf_op jit(solution)/shard_map/jit(_take)/gather | solution.py:52
  68.2 16.6 %gather_fusion.4 = bf16[256,2,3072]{2,1,0:T(2,128)(2,1)} fusion(bf16[625,2,3072]{2,1,0:T(2,128)(2,1)} %bitcast.86, s32[1024]{0:T(1024)S(1)} %pad_clamp_fusion.1), kind=kCustom, calls=%fused_computation.4.clone | custom fusion | bytes 6292480 | tf_op jit(solution)/shard_map/jit(_take)/gather | solution.py:50
  85.0 5.5 fusion.65
  90.5 5.5 fusion.63
  96.0 5.6 fusion.67
  101.6 240.8 %collective-permute-done = bf16[625,2,3072]{2,1,0:T(2,128)(2,1)} collective-permute-done((bf16[625,2,3072]{2,1,0:T(2,128)(2,1)}, bf16[625,2,3072]{2,1,0:T(2,128)(2,1)}, u32[]{:S(2)}, u32[]{:S(2)}) %collective-permute-start) | collective-permute-done | bytes 7680032 | tf_op jit(solution)/shard_map/ppermute | solution.py:16
  342.4 16.5 %gather_fusion.3 = bf16[256,2,3072]{2,1,0:T(2,128)(2,1)} fusion(bf16[625,2,3072]{2,1,0:T(2,128)(2,1)} %collective-permute-done, s32[1024]{0:T(1024)S(1)} %pad_clamp_fusion.2), kind=kCustom, calls=%fused_computation.3.clone | custom fusion | bytes 6292480 | tf_op jit(solution)/shard_map/jit(_take)/gather | solution.py:55
  358.9 7.6 fusion.66
  366.6 12.3 %add_convert_fusion.1 = (bf16[256,1,3072]{2,1,0:T(2,128)(2,1)S(1)}, bf16[256,1,3072]{2,1,0:T(2,128)(2,1)S(1)}) fusion(f32[256,2,3072]{2,1,0:T(2,128)} %fusion.66, f32[256,2,3072]{2,1,0:T(2,128)S(1)} %bitcast.80), kind=kLoop, calls=%fused_computation.85 | loop fusion | flops 6291456 | bytes 15728640 | tf_op jit(solution)/shard_map/convert.13
  379.8 1.9 pad_maximum_fusion.1
  381.9 118.2 %while.40 = (s32[]{:T(128)}, f32[4,512,256]{2,1,0:T(8,128)S(1)}, s32[4]{0:T(128)S(1)}, bf16[256,6144]{1,0:T(8,128)(2,1)}, s32[]{:T(128)}, /*index=5*/s32[]{:T(128)}) while((s32[]{:T(128)}, f32[4,512,256]{2,1,0:T(8,128)S(1)}, s32[4]{0:T(128)S(1)}, bf16[256,6144]{1,0:T(8,128)(2,1)}, s32[]{:T(128)}, /*index=5*/s32[]{:T(128)}) %tuple.118), condition=%wide.region_4.6_spmd.clone, body=%wide.region_3.5_spmd.clone.sunk | while | flops 1642208256 | bytes 28864632 | solution.py:77
  383.3 26.3 %cosine_convert_fusion.7 = (bf16[512,3072]{1,0:T(8,128)(2,1)S(1)}, bf16[512,3072]{1,0:T(8,128)(2,1)S(1)}) fusion(s32[3072]{0:T(1024)S(1)} %add_add_fusion.14, s32[512]{0:T(512)S(1)} %add_add_fusion.15), kind=kLoop, calls=%fused_computation.36.clone.1 | loop fusion | flops 18874368 | bytes 6305792 | tf_op jit(solution)/shard_map/convert.2
  409.6 1.8 fusion.119
  412.8 26.3 %cosine_convert_fusion.7 = (bf16[512,3072]{1,0:T(8,128)(2,1)S(1)}, bf16[512,3072]{1,0:T(8,128)(2,1)S(1)}) fusion(s32[3072]{0:T(1024)S(1)} %add_add_fusion.14, s32[512]{0:T(512)S(1)} %add_add_fusion.15), kind=kLoop, calls=%fused_computation.36.clone.1 | loop fusion | flops 18874368 | bytes 6305792 | tf_op jit(solution)/shard_map/convert.2
  439.2 1.8 fusion.119
  442.4 26.3 %cosine_convert_fusion.7 = (bf16[512,3072]{1,0:T(8,128)(2,1)S(1)}, bf16[512,3072]{1,0:T(8,128)(2,1)S(1)}) fusion(s32[3072]{0:T(1024)S(1)} %add_add_fusion.14, s32[512]{0:T(512)S(1)} %add_add_fusion.15), kind=kLoop, calls=%fused_computation.36.clone.1 | loop fusion | flops 18874368 | bytes 6305792 | tf_op jit(solution)/shard_map/convert.2
  468.7 1.8 fusion.119
  471.9 26.3 %cosine_convert_fusion.7 = (bf16[512,3072]{1,0:T(8,128)(2,1)S(1)}, bf16[512,3072]{1,0:T(8,128)(2,1)S(1)}) fusion(s32[3072]{0:T(1024)S(1)} %add_add_fusion.14, s32[512]{0:T(512)S(1)} %add_add_fusion.15), kind=kLoop, calls=%fused_computation.36.clone.1 | loop fusion | flops 18874368 | bytes 6305792 | tf_op jit(solution)/shard_map/convert.2
  498.3 1.8 fusion.119
  500.1 1.4 copy-done.3
  501.7 16.7 %gather_fusion.5 = bf16[256,2,3072]{2,1,0:T(2,128)(2,1)} fusion(bf16[625,2,3072]{2,1,0:T(2,128)(2,1)} %collective-permute-done.2, s32[1024]{0:T(1024)S(1)} %pad_clamp_fusion), kind=kCustom, calls=%fused_computation.5.clone | custom fusion | bytes 6292480 | tf_op jit(solution)/shard_map/jit(_take)/gather | solution.py:55
  518.4 7.6 fusion.68
  526.0 12.4 %add_convert_fusion = (bf16[256,1,3072]{2,1,0:T(2,128)(2,1)S(1)}, bf16[256,1,3072]{2,1,0:T(2,128)(2,1)S(1)}) fusion(f32[256,2,3072]{2,1,0:T(2,128)} %fusion.68, f32[256,2,3072]{2,1,0:T(2,128)S(1)} %bitcast.78), kind=kLoop, calls=%fused_computation.83 | loop fusion | flops 6291456 | bytes 15728640 | tf_op jit(solution)/shard_map/convert.9
  539.4 1.9 pad_maximum_fusion.2
  541.3 1.5 broadcast.191.clone
  542.8 121.2 %while.41 = (s32[]{:T(128)}, f32[4,512,256]{2,1,0:T(8,128)}, s32[4]{0:T(128)S(1)}, bf16[256,6144]{1,0:T(8,128)(2,1)}, s32[]{:T(128)}, /*index=5*/s32[]{:T(128)}) while((s32[]{:T(128)}, f32[4,512,256]{2,1,0:T(8,128)}, s32[4]{0:T(128)S(1)}, bf16[256,6144]{1,0:T(8,128)(2,1)}, s32[]{:T(128)}, /*index=5*/s32[]{:T(128)}) %tuple.132), condition=%wide.region_7.9_spmd.clone, body=%wide.region_6.8_spmd.clone.sunk | while | flops 1642208256 | bytes 28865140 | solution.py:77
  544.4 26.3 %cosine_convert_fusion.8 = (bf16[512,3072]{1,0:T(8,128)(2,1)S(1)}, bf16[512,3072]{1,0:T(8,128)(2,1)S(1)}) fusion(s32[3072]{0:T(1024)S(1)} %add_add_fusion.16, s32[512]{0:T(512)S(1)} %add_add_fusion.17), kind=kLoop, calls=%fused_computation.55.clone.1 | loop fusion | flops 18874368 | bytes 6305792 | tf_op jit(solution)/shard_map/convert.4
  570.7 2.6 fusion.122
  574.6 26.3 %cosine_convert_fusion.8 = (bf16[512,3072]{1,0:T(8,128)(2,1)S(1)}, bf16[512,3072]{1,0:T(8,128)(2,1)S(1)}) fusion(s32[3072]{0:T(1024)S(1)} %add_add_fusion.16, s32[512]{0:T(512)S(1)} %add_add_fusion.17), kind=kLoop, calls=%fused_computation.55.clone.1 | loop fusion | flops 18874368 | bytes 6305792 | tf_op jit(solution)/shard_map/convert.4
  601.0 2.6 fusion.122
  604.8 26.3 %cosine_convert_fusion.8 = (bf16[512,3072]{1,0:T(8,128)(2,1)S(1)}, bf16[512,3072]{1,0:T(8,128)(2,1)S(1)}) fusion(s32[3072]{0:T(1024)S(1)} %add_add_fusion.16, s32[512]{0:T(512)S(1)} %add_add_fusion.17), kind=kLoop, calls=%fused_computation.55.clone.1 | loop fusion | flops 18874368 | bytes 6305792 | tf_op jit(solution)/shard_map/convert.4
  631.2 2.6 fusion.122
  635.0 26.3 %cosine_convert_fusion.8 = (bf16[512,3072]{1,0:T(8,128)(2,1)S(1)}, bf16[512,3072]{1,0:T(8,128)(2,1)S(1)}) fusion(s32[3072]{0:T(1024)S(1)} %add_add_fusion.16, s32[512]{0:T(512)S(1)} %add_add_fusion.17), kind=kLoop, calls=%fused_computation.55.clone.1 | loop fusion | flops 18874368 | bytes 6305792 | tf_op jit(solution)/shard_map/convert.4
  661.4 2.6 fusion.122
  664.1 2.8 fusion.64
  667.0 12.0 %add_convert_fusion.2 = (bf16[256,1,3072]{2,1,0:T(2,128)(2,1)S(1)}, bf16[256,1,3072]{2,1,0:T(2,128)(2,1)S(1)}) fusion(f32[256,2,3072]{2,1,0:T(2,128)S(1)} %fusion.64, f32[256,2,3072]{2,1,0:T(2,128)} %fusion.63), kind=kLoop, calls=%fused_computation.87 | loop fusion | flops 6291456 | bytes 15728640 | tf_op jit(solution)/shard_map/convert.17
  682.1 1.9 pad_maximum_fusion
  684.0 5.8 fusion.75
  689.8 11.1 %reduce-scatter.8.cloned.1.call-done = f32[1024,256]{1,0:T(8,128)} async-done(((f32[2048,256]{1,0:T(8,128)}), f32[1024,256]{1,0:T(8,128)}) %reduce-scatter.8.cloned.1.call-update) | async-done | bytes 1048592 | tf_op jit(solution)/shard_map/reduce_scatter | solution.py:76
  701.0 5.7 fusion.81
  706.7 2.7 collective-permute-start.3
  709.6 117.7 %while.39 = (s32[]{:T(128)}, f32[4,512,256]{2,1,0:T(8,128)S(1)}, s32[4]{0:T(128)S(1)}, bf16[256,6144]{1,0:T(8,128)(2,1)}, s32[]{:T(128)}, /*index=5*/s32[]{:T(128)}) while((s32[]{:T(128)}, f32[4,512,256]{2,1,0:T(8,128)S(1)}, s32[4]{0:T(128)S(1)}, bf16[256,6144]{1,0:T(8,128)(2,1)}, s32[]{:T(128)}, /*index=5*/s32[]{:T(128)}) %tuple.133), condition=%wide.region_1.3_spmd.clone, body=%wide.region_0.0_spmd.clone.sunk | while | flops 1642208256 | bytes 28864632 | solution.py:77
  710.9 26.3 %cosine_convert_fusion.6 = (bf16[512,3072]{1,0:T(8,128)(2,1)S(1)}, bf16[512,3072]{1,0:T(8,128)(2,1)S(1)}) fusion(s32[3072]{0:T(1024)S(1)} %add_add_fusion.12, s32[512]{0:T(512)S(1)} %add_add_fusion.13), kind=kLoop, calls=%fused_computation.17.clone.1 | loop fusion | flops 18874368 | bytes 6305792 | tf_op jit(solution)/shard_map/convert
  737.2 1.8 fusion.116
  740.3 26.3 %cosine_convert_fusion.6 = (bf16[512,3072]{1,0:T(8,128)(2,1)S(1)}, bf16[512,3072]{1,0:T(8,128)(2,1)S(1)}) fusion(s32[3072]{0:T(1024)S(1)} %add_add_fusion.12, s32[512]{0:T(512)S(1)} %add_add_fusion.13), kind=kLoop, calls=%fused_computation.17.clone.1 | loop fusion | flops 18874368 | bytes 6305792 | tf_op jit(solution)/shard_map/convert
  766.6 1.8 fusion.116
  769.7 26.3 %cosine_convert_fusion.6 = (bf16[512,3072]{1,0:T(8,128)(2,1)S(1)}, bf16[512,3072]{1,0:T(8,128)(2,1)S(1)}) fusion(s32[3072]{0:T(1024)S(1)} %add_add_fusion.12, s32[512]{0:T(512)S(1)} %add_add_fusion.13), kind=kLoop, calls=%fused_computation.17.clone.1 | loop fusion | flops 18874368 | bytes 6305792 | tf_op jit(solution)/shard_map/convert
  796.1 1.8 fusion.116
  799.2 26.3 %cosine_convert_fusion.6 = (bf16[512,3072]{1,0:T(8,128)(2,1)S(1)}, bf16[512,3072]{1,0:T(8,128)(2,1)S(1)}) fusion(s32[3072]{0:T(1024)S(1)} %add_add_fusion.12, s32[512]{0:T(512)S(1)} %add_add_fusion.13), kind=kLoop, calls=%fused_computation.17.clone.1 | loop fusion | flops 18874368 | bytes 6305792 | tf_op jit(solution)/shard_map/convert
  825.5 1.8 fusion.116
  827.4 1.3 copy-done.4
  829.6 1.3 fusion.94
  830.8 32.4 %reduce-scatter.4.cloned.1.call-done = f32[1024,256]{1,0:T(8,128)} async-done(((f32[2048,256]{1,0:T(8,128)}), f32[1024,256]{1,0:T(8,128)}) %reduce-scatter.4.cloned.1.call-update) | async-done | bytes 1048592 | tf_op jit(solution)/shard_map/reduce_scatter | solution.py:76
  863.3 3.6 fusion.70
  866.9 2.3 fusion.78
  869.1 47.5 %collective-permute-done.3 = f32[1250,1024]{1,0:T(8,128)} collective-permute-done((f32[1250,1024]{1,0:T(8,128)}, f32[1250,1024]{1,0:T(8,128)}, u32[]{:S(2)}, u32[]{:S(2)}) %collective-permute-start.3) | collective-permute-done | bytes 5120032 | tf_op jit(solution)/shard_map/ppermute | solution.py:16
  916.6 9.4 add_bitcast_fusion
  926.0 132.1 %all-gather.4.cloned.1.call-done = f32[4,1250,1024]{2,1,0:T(8,128)} async-done(((f32[1,1250,1024]{2,1,0:T(8,128)}), f32[4,1250,1024]{2,1,0:T(8,128)}) %all-gather.4.cloned.1.call-update) | async-done | bytes 20480016 | tf_op jit(solution)/shard_map/all_gather | solution.py:98
  1058.1 10.3 reduce_sum.9
  1068.5 7.3 reshape.172
  (134 shorter events, 26.1 us)
Async XLA Ops:
  6.5 677.5 %reduce-scatter.6.cloned.1.call-start = ((), (), s32[]{:S(2)}) async-start(), calls=%async_computation.4 | async-start | bytes 3145728 | tf_op jit(solution)/shard_map/reduce_scatter | solution.py:76
  6.5 335.9 %collective-permute-start = (bf16[625,2,3072]{2,1,0:T(2,128)(2,1)}, bf16[625,2,3072]{2,1,0:T(2,128)(2,1)}, u32[]{:S(2)}, u32[]{:S(2)}) collective-permute-start(bf16[625,2,3072]{2,1,0:T(2,128)(2,1)} %bitcast.81), channel_id=1, source_target_pairs={{8,0},{16,8},{24,16},{32,24},{40,32},{48,40},{56,48},{64,56},{72,6... | collective-permute-start | bytes 23040008 | tf_op jit(solution)/shard_map/ppermute | solution.py:16
  13.6 488.1 %collective-permute-start.2 = (bf16[625,2,3072]{2,1,0:T(2,128)(2,1)}, bf16[625,2,3072]{2,1,0:T(2,128)(2,1)}, u32[]{:S(2)}, u32[]{:S(2)}) collective-permute-start(bf16[625,2,3072]{2,1,0:T(2,128)(2,1)} %bitcast.82), channel_id=1, source_target_pairs={{16,0},{24,8},{32,16},{40,24},{48,32},{56,40},{64,48},{72,56},{80,... | collective-permute-start | bytes 23040008 | tf_op jit(solution)/shard_map/ppermute | solution.py:16
  85.0 5.5 copy-start.1
  90.5 5.5 copy-start.2
  342.4 24.1 %slice-start.2 = ((s8[6291456]{0:T(1024)(128)(4,1)}), s8[2097152]{0:T(1024)(128)(4,1)S(1)}, s32[]{:S(2)}) async-start(s8[6291456]{0:T(1024)(128)(4,1)} %bitcast.79), calls=%async_computation.9 | async-start | bytes 4194304
  358.9 7.6 slice-start.3
  383.3 26.3 %copy-start.8 = (bf16[256,6144]{1,0:T(8,128)(2,1)S(1)}, bf16[256,6144]{1,0:T(8,128)(2,1)}, u32[]{:S(2)}) copy-start(bf16[256,6144]{1,0:T(8,128)(2,1)} %get-tuple-element.467) | copy-start | bytes 9437188 | tf_op jit(solution)/shard_map/while
  412.8 26.3 %copy-start.8 = (bf16[256,6144]{1,0:T(8,128)(2,1)S(1)}, bf16[256,6144]{1,0:T(8,128)(2,1)}, u32[]{:S(2)}) copy-start(bf16[256,6144]{1,0:T(8,128)(2,1)} %get-tuple-element.467) | copy-start | bytes 9437188 | tf_op jit(solution)/shard_map/while
  442.4 26.3 %copy-start.8 = (bf16[256,6144]{1,0:T(8,128)(2,1)S(1)}, bf16[256,6144]{1,0:T(8,128)(2,1)}, u32[]{:S(2)}) copy-start(bf16[256,6144]{1,0:T(8,128)(2,1)} %get-tuple-element.467) | copy-start | bytes 9437188 | tf_op jit(solution)/shard_map/while
  471.9 26.3 %copy-start.8 = (bf16[256,6144]{1,0:T(8,128)(2,1)S(1)}, bf16[256,6144]{1,0:T(8,128)(2,1)}, u32[]{:S(2)}) copy-start(bf16[256,6144]{1,0:T(8,128)(2,1)} %get-tuple-element.467) | copy-start | bytes 9437188 | tf_op jit(solution)/shard_map/while
  500.1 1.4 copy-start.3
  501.6 199.4 %reduce-scatter.8.cloned.1.call-start = ((), (), s32[]{:S(2)}) async-start(), calls=%async_computation.5 | async-start | bytes 3145728 | tf_op jit(solution)/shard_map/reduce_scatter | solution.py:76
  501.7 24.3 %slice-start = ((s8[6291456]{0:T(1024)(128)(4,1)}), s8[2097152]{0:T(1024)(128)(4,1)S(1)}, s32[]{:S(2)}) async-start(s8[6291456]{0:T(1024)(128)(4,1)} %bitcast.77), calls=%async_computation.7 | async-start | bytes 4194304
  518.4 7.6 slice-start.1
  542.8 121.3 %copy-start = (bf16[256,2,3072]{2,1,0:T(2,128)(2,1)S(1)}, bf16[256,2,3072]{2,1,0:T(2,128)(2,1)}, u32[]{:S(2)}) copy-start(bf16[256,2,3072]{2,1,0:T(2,128)(2,1)} %gather_fusion.1) | copy-start | bytes 9437188
  544.4 26.3 %copy-start.9 = (bf16[256,6144]{1,0:T(8,128)(2,1)S(1)}, bf16[256,6144]{1,0:T(8,128)(2,1)}, u32[]{:S(2)}) copy-start(bf16[256,6144]{1,0:T(8,128)(2,1)} %get-tuple-element.449) | copy-start | bytes 9437188 | tf_op jit(solution)/shard_map/while
  574.6 26.3 %copy-start.9 = (bf16[256,6144]{1,0:T(8,128)(2,1)S(1)}, bf16[256,6144]{1,0:T(8,128)(2,1)}, u32[]{:S(2)}) copy-start(bf16[256,6144]{1,0:T(8,128)(2,1)} %get-tuple-element.449) | copy-start | bytes 9437188 | tf_op jit(solution)/shard_map/while
  604.8 26.3 %copy-start.9 = (bf16[256,6144]{1,0:T(8,128)(2,1)S(1)}, bf16[256,6144]{1,0:T(8,128)(2,1)}, u32[]{:S(2)}) copy-start(bf16[256,6144]{1,0:T(8,128)(2,1)} %get-tuple-element.449) | copy-start | bytes 9437188 | tf_op jit(solution)/shard_map/while
  635.0 26.3 %copy-start.9 = (bf16[256,6144]{1,0:T(8,128)(2,1)S(1)}, bf16[256,6144]{1,0:T(8,128)(2,1)}, u32[]{:S(2)}) copy-start(bf16[256,6144]{1,0:T(8,128)(2,1)} %get-tuple-element.449) | copy-start | bytes 9437188 | tf_op jit(solution)/shard_map/while
  664.0 199.2 %reduce-scatter.4.cloned.1.call-start = ((), (), s32[]{:S(2)}) async-start(), calls=%async_computation.3 | async-start | bytes 3145728 | tf_op jit(solution)/shard_map/reduce_scatter | solution.py:76
  679.5 0.7 copy-start.15
  689.8 179.3 %collective-permute-start.1 = (f32[1250,1024]{1,0:T(8,128)}, f32[1250,1024]{1,0:T(8,128)}, u32[]{:S(2)}, u32[]{:S(2)}) collective-permute-start(f32[1250,1024]{1,0:T(8,128)} %fusion.75), channel_id=1, source_target_pairs={{120,0},{0,8},{8,16},{16,24},{24,32},{32,40},{40,48},{48,56},{56,6... | collective-permute-start | bytes 15360008 | tf_op jit(solution)/shard_map/ppermute | solution.py:16
  706.7 209.9 %collective-permute-start.3 = (f32[1250,1024]{1,0:T(8,128)}, f32[1250,1024]{1,0:T(8,128)}, u32[]{:S(2)}, u32[]{:S(2)}) collective-permute-start(f32[1250,1024]{1,0:T(8,128)} %fusion.81), channel_id=1, source_target_pairs={{112,0},{120,8},{0,16},{8,24},{16,32},{24,40},{32,48},{40,56},{48,... | collective-permute-start | bytes 15360008 | tf_op jit(solution)/shard_map/ppermute | solution.py:16
  709.6 120.0 %copy-start.13 = (pred[256]{0:T(512)(128)(4,1)S(1)}, pred[256]{0:T(512)(128)(4,1)}, u32[]{:S(2)}) copy-start(pred[256]{0:T(512)(128)(4,1)} %get-tuple-element.249) | copy-start | bytes 772
  709.6 120.0 %copy-start.14 = (pred[256]{0:T(512)(128)(4,1)S(1)}, pred[256]{0:T(512)(128)(4,1)}, u32[]{:S(2)}) copy-start(pred[256]{0:T(512)(128)(4,1)} %get-tuple-element.253) | copy-start | bytes 772
  709.6 153.6 %copy-start.11 = (s32[256]{0:T(256)S(1)}, s32[256]{0:T(256)}, u32[]{:S(2)}) copy-start(s32[256]{0:T(256)} %get-tuple-element.312) | copy-start | bytes 3076
  710.9 26.3 %copy-start.7 = (bf16[256,6144]{1,0:T(8,128)(2,1)S(1)}, bf16[256,6144]{1,0:T(8,128)(2,1)}, u32[]{:S(2)}) copy-start(bf16[256,6144]{1,0:T(8,128)(2,1)} %get-tuple-element.485) | copy-start | bytes 9437188 | tf_op jit(solution)/shard_map/while
  740.3 26.3 %copy-start.7 = (bf16[256,6144]{1,0:T(8,128)(2,1)S(1)}, bf16[256,6144]{1,0:T(8,128)(2,1)}, u32[]{:S(2)}) copy-start(bf16[256,6144]{1,0:T(8,128)(2,1)} %get-tuple-element.485) | copy-start | bytes 9437188 | tf_op jit(solution)/shard_map/while
  769.7 26.3 %copy-start.7 = (bf16[256,6144]{1,0:T(8,128)(2,1)S(1)}, bf16[256,6144]{1,0:T(8,128)(2,1)}, u32[]{:S(2)}) copy-start(bf16[256,6144]{1,0:T(8,128)(2,1)} %get-tuple-element.485) | copy-start | bytes 9437188 | tf_op jit(solution)/shard_map/while
  799.2 26.3 %copy-start.7 = (bf16[256,6144]{1,0:T(8,128)(2,1)S(1)}, bf16[256,6144]{1,0:T(8,128)(2,1)}, u32[]{:S(2)}) copy-start(bf16[256,6144]{1,0:T(8,128)(2,1)} %get-tuple-element.485) | copy-start | bytes 9437188 | tf_op jit(solution)/shard_map/while
  827.4 1.3 copy-start.4
  828.7 229.4 %all-gather.4.cloned.1.call-start = ((), (), s32[]{:S(2)}) async-start(), calls=%async_computation.6 | async-start | bytes 25722880 | tf_op jit(solution)/shard_map/all_gather | solution.py:98
  863.3 3.6 copy-start.6
  863.3 3.6 copy-start.10
  866.8 49.8 %copy-start.5 = (f32[1024,256]{1,0:T(8,128)S(1)}, f32[1024,256]{1,0:T(8,128)}, u32[]{:S(2)}) copy-start(f32[1024,256]{1,0:T(8,128)} %reduce-scatter.6.cloned.1.call-done) | copy-start | bytes 3145732
  866.9 49.7 %copy-start.12 = (s32[256]{0:T(256)S(1)}, s32[256]{0:T(256)}, u32[]{:S(2)}) copy-start(s32[256]{0:T(256)} %get-tuple-element.308) | copy-start | bytes 3076
Sparse Core Ops, SparseCore 0:
  501.7 36.7 reduce-scatter.5
  664.2 36.7 reduce-scatter.7
  828.8 34.3 reduce-scatter.3
  926.1 131.9 all-gather.3
